TPU v7x, 32 devices: a whole 2x2x4 slice. The times are simulated.
32 devices in a mesh: pts: 8 (over y, x, core), cen: 4 (over z).
Axes of the slice: x: 2, y: 2, z: 4, core: 2. Of those that a mesh axis runs over, the one named last changes fastest.
Arguments:
- embeddings: float32 [8192, 64], P('pts'), may hold values from -0.75 to 0.75
- centroids: float32 [8192, 64], P('cen'), may hold values from -0.75 to 0.75
- point_duals: float32 [8192], P('pts'), may hold values from -4 to 0.1
- centroid_duals: float32 [8192], P('cen'), may hold values from -1.5 to 2.6
- targets: float32 [8192, 64], P('pts'), may hold values from -6 to 6
Outputs:
- grad_emb: float32 [8192, 64], P('pts')
- grad_cen: float32 [8192, 64], P(('cen', 'pts'))
All inputs are finite; a program needn't handle non-finite values.
Results may differ from a plain program's by a relative error of at most 0.0003.
Values sent between devices are 32-bit elements; how exact they have to be, the bound alone decides.
No kernel may reach another device: no remote copies, remote signals or barrier semaphores. Data moves between devices by JAX's collectives and lax.ppermute only.
A program may use at most 64 MiB of HBM per device.

v0:
```python
import jax
import jax.numpy as jnp
from jax import lax
from jax.sharding import PartitionSpec as P

ITERS = 3
EPSILON = 0.08


def plan_block(points, duals_row, cen_block, duals_block, plan_total):
    scores = jnp.dot(
        points, cen_block.T, precision=lax.Precision.HIGHEST, preferred_element_type=jnp.float32
    )
    return jnp.exp(duals_row[:, None] + duals_block[None, :] + scores / EPSILON) / plan_total


def shards(embeddings, centroids, point_duals, centroid_duals, targets):
    exact_mode = lax.Precision.HIGHEST
    cen_rows, feat_width = centroids.shape
    plan_total = float(cen_rows * lax.axis_size("cen"))
    block_cols = min(256, cen_rows)
    block_count = cen_rows // block_cols
    cen_blocks = centroids.reshape(block_count, block_cols, feat_width)
    dual_blocks = centroid_duals.reshape(block_count, block_cols)
    rows_zero = jnp.zeros(point_duals.shape, jnp.float32)

    def first_step(running, inputs):
        cen_block, duals_block = inputs
        plan_tile = plan_block(embeddings, point_duals, cen_block, duals_block, plan_total)
        target_scores = jnp.dot(
            targets, cen_block.T, precision=exact_mode, preferred_element_type=jnp.float32
        )
        weighted = plan_tile * target_scores
        return (
            (running[0] + plan_tile.sum(1), running[1] + weighted.sum(1)),
            (plan_tile.sum(0), weighted.sum(0)),
        )

    (row_mass, row_load), (col_mass, col_load) = lax.scan(
        first_step, (rows_zero, rows_zero), (cen_blocks, dual_blocks)
    )
    col_mass = col_mass.reshape(-1)
    col_load = col_load.reshape(-1)
    row_mass, row_load = lax.psum((row_mass, row_load), "cen")
    col_mass, col_load = lax.psum((col_mass, col_load), "pts")
    col_scale = col_load / col_mass
    row_scale = row_load / row_mass
    for sweep_turn in range(ITERS):
        adjoint_scale_blocks = col_scale.reshape(block_count, block_cols)

        def sweep_step(running, inputs):
            cen_block, duals_block, scale_block = inputs
            plan_tile = plan_block(embeddings, point_duals, cen_block, duals_block, plan_total)
            row_part = jnp.dot(
                plan_tile, scale_block, precision=exact_mode, preferred_element_type=jnp.float32
            )
            col_part = jnp.dot(
                row_scale, plan_tile, precision=exact_mode, preferred_element_type=jnp.float32
            )
            return (running + row_part, col_part)

        row_terms, col_terms = lax.scan(
            sweep_step, rows_zero, (cen_blocks, dual_blocks, adjoint_scale_blocks)
        )
        row_terms, col_terms = (row_terms, col_terms.reshape(-1))
        row_terms = lax.psum(row_terms, "cen")
        col_terms = lax.psum(col_terms, "pts")
        col_scale = (col_load - col_terms) / col_mass
        row_scale = (row_load - row_terms) / row_mass
    scale_blocks = col_scale.reshape(block_count, block_cols)
    emb_zero = jnp.zeros((embeddings.shape[0], feat_width), jnp.float32)

    def block_weights(cen_block, duals_block, scale_block):
        plan_tile = plan_block(embeddings, point_duals, cen_block, duals_block, plan_total)
        target_scores = jnp.dot(
            targets, cen_block.T, precision=exact_mode, preferred_element_type=jnp.float32
        )
        return plan_tile * (target_scores - row_scale[:, None] - scale_block[None, :])

    def final_step(running, inputs):
        cen_block, duals_block, scale_block = inputs
        weights = block_weights(cen_block, duals_block, scale_block)
        emb_part = jnp.dot(
            weights, cen_block, precision=exact_mode, preferred_element_type=jnp.float32
        )
        cen_part = lax.dot_general(
            weights,
            embeddings,
            (((0,), (0,)), ((), ())),
            precision=exact_mode,
            preferred_element_type=jnp.float32,
        )
        return (running + emb_part, cen_part)

    emb_local, cen_parts = lax.scan(final_step, emb_zero, (cen_blocks, dual_blocks, scale_blocks))
    grad_cen = lax.psum_scatter(
        cen_parts.reshape(cen_rows, feat_width), "pts", scatter_dimension=0, tiled=True
    )
    grad_emb = lax.psum(emb_local, "cen")
    return (grad_emb, grad_cen)


def solution(mesh):
    in_specs = (P("pts", None), P("cen", None), P("pts"), P("cen"), P("pts", None))
    out_specs = (P("pts", None), P(("cen", "pts"), None))
    return jax.shard_map(shards, mesh=mesh, in_specs=in_specs, out_specs=out_specs, check_vma=False)
```

profile of v0, /device:TPU:0, one launch (start us, length us, event | category | flops | bytes accessed | tf_op | source)
XLA Modules:
  0.0 287.0 jit_solution(17219121614646234759)
XLA Ops:
  8.8 1.4 copy.7
  10.9 20.4 %while.69 = (s32[]{:T(128)}, f32[1024]{0:T(1024)S(1)}, f32[1024]{0:T(1024)S(1)}, f32[8,256]{1,0:T(8,128)S(1)}, f32[8,256]{1,0:T(8,128)S(1)}, /*index=5*/f32[1024...) while((s32[]{:T(128)}, f32[1024]{0:T(1024)S(1)}, ...), condition=%wide.region_5.6_spmd.clone, body=%wide.region_0.5_spmd.clone.sunk | while | flops 405014016 | bytes 2929819 | solution.py:39
  10.9 1.3 fusion.127
  13.5 1.3 fusion.127
  14.8 1.1 fusion.128
  16.0 1.3 fusion.127
  17.3 1.1 fusion.128
  18.6 1.3 fusion.127
  19.9 1.1 fusion.128
  21.1 1.3 fusion.127
  22.4 1.1 fusion.128
  23.7 1.3 fusion.127
  25.0 1.1 fusion.128
  26.2 1.3 fusion.127
  27.5 1.1 fusion.128
  28.8 1.3 fusion.127
  30.1 1.1 fusion.128
  31.3 25.5 %all-reduce = (f32[2048]{0:T(1024)S(1)}, f32[2048]{0:T(1024)S(1)}) all-reduce(f32[2048]{0:T(1024)S(1)} %bitcast.258, f32[2048]{0:T(1024)S(1)} %bitcast.259), channel_id=1, replica_groups=mesh['pts'=8,'cen'=4] {'pts'}, use_global_device_ids=true, to_apply=%region_7.8 | all-reduce | flops 4096 | bytes 32768 | tf_op jit(solution)/shard_map/psum | solution.py:45
  56.9 12.1 %all-reduce.1 = (f32[1024]{0:T(1024)S(1)}, f32[1024]{0:T(1024)S(1)}) all-reduce(f32[1024]{0:T(1024)S(1)} %get-tuple-element.257, f32[1024]{0:T(1024)S(1)} %get-tuple-element.254), channel_id=1, replica_groups=mesh['pts'=8,'cen'=4] {'cen'}, use_global_device_ids=true, to_apply=%region_9.10 | all-reduce | flops 2048 | bytes 16384 | tf_op jit(solution)/shard_map/psum | solution.py:44
  69.0 22.4 %while.70 = (s32[]{:T(128)}, f32[1024]{0:T(1024)S(1)}, f32[8,256]{1,0:T(8,128)S(1)}, f32[1024]{0:T(1024)S(1)}, f32[8,256]{1,0:T(8,128)S(1)}, /*index=5*/f32[8,25...) while((s32[]{:T(128)}, f32[1024]{0:T(1024)S(1)}, ...), condition=%wide.region_11.12_spmd.clone, body=%wide.region_10.11_spmd.clone.sunk | while | flops 208668672 | bytes 3570831 | solution.py:62
  69.1 1.1 fusion.135
  71.9 1.1 fusion.135
  74.7 1.1 fusion.135
  77.5 1.1 fusion.135
  80.3 1.1 fusion.135
  83.1 1.1 fusion.135
  85.9 1.1 fusion.135
  88.7 1.1 fusion.135
  91.5 12.1 %psum.81 = f32[2048]{0:T(1024)S(1)} all-reduce(f32[2048]{0:T(1024)S(1)} %bitcast.260), channel_id=1, replica_groups=mesh['pts'=8,'cen'=4] {'pts'}, use_global_device_ids=true, to_apply=%region_12.13 | all-reduce | flops 2048 | bytes 16384 | tf_op jit(solution)/shard_map/psum | solution.py:67
  103.6 8.4 %psum.82 = f32[1024]{0:T(1024)S(1)} all-reduce(f32[1024]{0:T(1024)S(1)} %get-tuple-element.259), channel_id=1, replica_groups=mesh['pts'=8,'cen'=4] {'cen'}, use_global_device_ids=true, to_apply=%region_13.14 | all-reduce | flops 1024 | bytes 8192 | tf_op jit(solution)/shard_map/psum | solution.py:66
  112.0 22.4 %while.71 = (s32[]{:T(128)}, f32[1024]{0:T(1024)S(1)}, f32[8,256]{1,0:T(8,128)S(1)}, f32[1024]{0:T(1024)S(1)}, f32[8,256]{1,0:T(8,128)S(1)}, /*index=5*/f32[8,25...) while((s32[]{:T(128)}, f32[1024]{0:T(1024)S(1)}, ...), condition=%wide.region_15.16_spmd.clone, body=%wide.region_14.15_spmd.clone.sunk | while | flops 208668672 | bytes 3570831 | solution.py:62
  112.1 1.1 fusion.144
  114.9 1.1 fusion.144
  117.7 1.1 fusion.144
  120.5 1.1 fusion.144
  123.3 1.1 fusion.144
  126.1 1.1 fusion.144
  128.9 1.1 fusion.144
  131.7 1.1 fusion.144
  134.5 12.1 %psum.83 = f32[2048]{0:T(1024)S(1)} all-reduce(f32[2048]{0:T(1024)S(1)} %bitcast.261), channel_id=1, replica_groups=mesh['pts'=8,'cen'=4] {'pts'}, use_global_device_ids=true, to_apply=%region_16.17 | all-reduce | flops 2048 | bytes 16384 | tf_op jit(solution)/shard_map/psum | solution.py:67
  146.6 10.4 %psum.84 = f32[1024]{0:T(1024)S(1)} all-reduce(f32[1024]{0:T(1024)S(1)} %get-tuple-element.261), channel_id=1, replica_groups=mesh['pts'=8,'cen'=4] {'cen'}, use_global_device_ids=true, to_apply=%region_17.18 | all-reduce | flops 1024 | bytes 8192 | tf_op jit(solution)/shard_map/psum | solution.py:66
  157.0 22.4 %while.72 = (s32[]{:T(128)}, f32[1024]{0:T(1024)S(1)}, f32[8,256]{1,0:T(8,128)S(1)}, f32[1024]{0:T(1024)S(1)}, f32[8,256]{1,0:T(8,128)S(1)}, /*index=5*/f32[8,25...) while((s32[]{:T(128)}, f32[1024]{0:T(1024)S(1)}, ...), condition=%wide.region_19.20_spmd.clone, body=%wide.region_18.19_spmd.clone.sunk | while | flops 208668672 | bytes 3570831 | solution.py:62
  157.0 1.1 fusion.153
  159.9 1.1 fusion.153
  162.7 1.1 fusion.153
  165.5 1.1 fusion.153
  168.3 1.1 fusion.153
  171.1 1.1 fusion.153
  173.9 1.1 fusion.153
  176.7 1.1 fusion.153
  179.5 8.4 %psum.85 = f32[1024]{0:T(1024)S(1)} all-reduce(f32[1024]{0:T(1024)S(1)} %get-tuple-element.262), channel_id=1, replica_groups=mesh['pts'=8,'cen'=4] {'cen'}, use_global_device_ids=true, to_apply=%region_21.22 | all-reduce | flops 1024 | bytes 8192 | tf_op jit(solution)/shard_map/psum | solution.py:66
  187.9 12.3 %psum.86 = f32[2048]{0:T(1024)S(1)} all-reduce(f32[2048]{0:T(1024)S(1)} %bitcast.262), channel_id=1, replica_groups=mesh['pts'=8,'cen'=4] {'pts'}, use_global_device_ids=true, to_apply=%region_20.21 | all-reduce | flops 2048 | bytes 16384 | tf_op jit(solution)/shard_map/psum | solution.py:67
  200.2 40.8 %while.73 = (s32[]{:T(128)}, f32[1024,64]{0,1:T(8,128)S(1)}, f32[8,256,64]{1,0,2:T(8,128)S(1)}, f32[1024]{0:T(1024)S(1)}, f32[8,256]{1,0:T(8,128)S(1)}, /*index=...) while((s32[]{:T(128)}, f32[1024,64]{0,1:T(8,128)S(1)}, ...), condition=%wide.region_23.24_spmd.clone, body=%wide.region_22.23_spmd.clone.sunk | while | flops 807272448 | bytes 7288987 | solution.py:95
  200.2 1.1 fusion.164
  205.3 1.1 fusion.164
  210.4 1.1 fusion.164
  215.5 1.1 fusion.164
  220.6 1.1 fusion.164
  225.7 1.1 fusion.164
  230.8 1.1 fusion.164
  235.9 1.1 fusion.164
  242.8 32.5 %all-reduce.4.cloned.1.call-done = f32[1024,64]{0,1:T(8,128)} async-done(((f32[1024,64]{0,1:T(8,128)}), f32[1024,64]{0,1:T(8,128)}) %all-reduce.4.cloned.1.call-update) | async-done | bytes 262160 | tf_op jit(solution)/shard_map/psum | solution.py:99
  275.3 2.5 reduce-scatter.2.cloned.1.call-done
  277.8 1.7 copy.77
  (246 shorter events, 75.6 us)
Async XLA Ops:
  8.0 267.3 %all-reduce.4.cloned.1.call-start = ((), (), s32[]{:S(2)}) async-start(), calls=%async_computation.1 | async-start | bytes 524288 | tf_op jit(solution)/shard_map/psum | solution.py:99
  8.1 0.7 copy-start.4
  8.8 1.5 copy-start
  8.8 1.5 copy-start.1
  10.2 0.7 copy-start.3
  241.0 0.7 copy-start.2
  241.8 36.1 %reduce-scatter.2.cloned.1.call-start = ((), (), s32[]{:S(2)}) async-start(), calls=%async_computation.2 | async-start | bytes 589824 | tf_op jit(solution)/shard_map/reduce_scatter | solution.py:96
Sparse Core Ops, SparseCore 0:
  241.9 33.3 all-reduce.3
Sparse Core Ops, SparseCore 1:
  245.9 31.9 reduce-scatter.1
where the time goes:
time: 287 us
  matrix products  117 us (41%)
  blocking collectives  101 us (35%)
  waiting for transfers between devices  35.1 us (12%)
  between operations  15.8 us (6%)
  local copies, waits for them, and re-layouts  15.5 us (5%)
    dot_general x40, matrix products, plan_block(): jnp.dot(points, cen_block.T, precision=lax.Precision.HIGHEST, preferred_e...  46.6 us
    psum x3, blocking collectives, shards(): col_terms = lax.psum(col_terms, 'pts')  36.5 us
    psum x1, waiting for transfers between devices, shards(): grad_emb = lax.psum(emb_local, 'cen')  32.5 us
    psum x3, blocking collectives, shards(): row_terms = lax.psum(row_terms, 'cen')  27.1 us
    psum x1, blocking collectives, shards(): col_mass, col_load = lax.psum((col_mass, col_load), 'pts')  25.5 us
    dot_general x24, matrix products, sweep_step(): jnp.dot(row_scale, plan_tile, precision=exact_mode, preferred_element_typ...  22 us
    dot_general x24, matrix products, sweep_step(): jnp.dot(plan_tile, scale_block, precision=exact_mode, preferred_element_t...  16.1 us
    psum x1, blocking collectives, shards(): row_mass, row_load = lax.psum((row_mass, row_load), 'cen')  12.1 us
  transfers between devices with their start and end apart: 2, of which 2 were waited for; matrix products, arithmetic and copies ran while one was open for 0% of the time, Pallas kernels for 0%

commit v1 on v0

--- a/solution.py
+++ b/solution.py
@@ -64,7 +64,8 @@
         )
         row_terms, col_terms = (row_terms, col_terms.reshape(-1))
         row_terms = lax.psum(row_terms, "cen")
-        col_terms = lax.psum(col_terms, "pts")
+        parts = lax.all_gather(col_terms, "pts", axis=0, tiled=False)
+        col_terms = parts.sum(axis=0)
         col_scale = (col_load - col_terms) / col_mass
         row_scale = (row_load - row_terms) / row_mass
     scale_blocks = col_scale.reshape(block_count, block_cols)

time: 287 us -> 278 us (0.969)
  blocking collectives: 101 us -> 90.5 us
    psum x3 -> x0, blocking collectives: 36.5 us -> none  [shards(): col_terms = lax.psum(col_terms, 'pts')]
    all_gather x0 -> x3, blocking collectives: none -> 25.7 us  [shards(): parts = lax.all_gather(col_terms, 'pts', axis=0, tiled=False)]
where the time goes in v1:
time: 278 us; the launch traced here: 277 us
  matrix products  117 us (42%)
  blocking collectives  90.5 us (33%)
  waiting for transfers between devices  36 us (13%)
  between operations  15.7 us (6%)
  local copies, waits for them, and re-layouts  15.6 us (6%)
    dot_general x40, matrix products, plan_block(): jnp.dot(points, cen_block.T, precision=lax.Precision.HIGHEST, preferred_e...  46.6 us
    psum x1, waiting for transfers between devices, shards(): grad_emb = lax.psum(emb_local, 'cen')  33.5 us
    psum x3, blocking collectives, shards(): row_terms = lax.psum(row_terms, 'cen')  27.1 us
    all_gather x3, blocking collectives, shards(): parts = lax.all_gather(col_terms, 'pts', axis=0, tiled=False)  25.7 us
    psum x1, blocking collectives, shards(): col_mass, col_load = lax.psum((col_mass, col_load), 'pts')  25.5 us
    dot_general x24, matrix products, sweep_step(): jnp.dot(row_scale, plan_tile, precision=exact_mode, preferred_element_typ...  22 us
    dot_general x24, matrix products, sweep_step(): jnp.dot(plan_tile, scale_block, precision=exact_mode, preferred_element_t...  16.1 us
    psum x1, blocking collectives, shards(): row_mass, row_load = lax.psum((row_mass, row_load), 'cen')  12.1 us
  transfers between devices with their start and end apart: 2, of which 2 were waited for; matrix products, arithmetic and copies ran while one was open for 0% of the time, Pallas kernels for 0%

profile of v1, /device:TPU:0, one launch (start us, length us, event | category | flops | bytes accessed | tf_op | source)
XLA Modules:
  0.0 277.2 jit_solution(3084939179725667392)
XLA Ops:
  8.8 1.4 copy.9
  10.9 20.4 %while.69 = (s32[]{:T(128)}, f32[1024]{0:T(1024)S(1)}, f32[1024]{0:T(1024)S(1)}, f32[8,256]{1,0:T(8,128)S(1)}, f32[8,256]{1,0:T(8,128)S(1)}, /*index=5*/f32[1024...) while((s32[]{:T(128)}, f32[1024]{0:T(1024)S(1)}, ...), condition=%wide.region_5.6_spmd.clone, body=%wide.region_0.5_spmd.clone.sunk | while | flops 405014016 | bytes 2929819 | solution.py:39
  10.9 1.3 fusion.127
  13.5 1.3 fusion.127
  14.8 1.1 fusion.128
  16.0 1.3 fusion.127
  17.3 1.1 fusion.128
  18.6 1.3 fusion.127
  19.9 1.1 fusion.128
  21.1 1.3 fusion.127
  22.4 1.1 fusion.128
  23.7 1.3 fusion.127
  25.0 1.1 fusion.128
  26.2 1.3 fusion.127
  27.5 1.1 fusion.128
  28.8 1.3 fusion.127
  30.1 1.1 fusion.128
  31.3 25.5 %all-reduce = (f32[2048]{0:T(1024)S(1)}, f32[2048]{0:T(1024)S(1)}) all-reduce(f32[2048]{0:T(1024)S(1)} %bitcast.249, f32[2048]{0:T(1024)S(1)} %bitcast.250), channel_id=1, replica_groups=mesh['pts'=8,'cen'=4] {'pts'}, use_global_device_ids=true, to_apply=%region_7.8 | all-reduce | flops 4096 | bytes 32768 | tf_op jit(solution)/shard_map/psum | solution.py:45
  56.9 12.1 %all-reduce.1 = (f32[1024]{0:T(1024)S(1)}, f32[1024]{0:T(1024)S(1)}) all-reduce(f32[1024]{0:T(1024)S(1)} %get-tuple-element.257, f32[1024]{0:T(1024)S(1)} %get-tuple-element.254), channel_id=1, replica_groups=mesh['pts'=8,'cen'=4] {'cen'}, use_global_device_ids=true, to_apply=%region_9.10 | all-reduce | flops 2048 | bytes 16384 | tf_op jit(solution)/shard_map/psum | solution.py:44
  69.0 22.4 %while.70 = (s32[]{:T(128)}, f32[1024]{0:T(1024)S(1)}, f32[8,256]{1,0:T(8,128)S(1)}, f32[1024]{0:T(1024)S(1)}, f32[8,256]{1,0:T(8,128)S(1)}, /*index=5*/f32[8,25...) while((s32[]{:T(128)}, f32[1024]{0:T(1024)S(1)}, ...), condition=%wide.region_11.12_spmd.clone, body=%wide.region_10.11_spmd.clone.sunk | while | flops 208668672 | bytes 3570831 | solution.py:62
  69.1 1.1 fusion.135
  71.9 1.1 fusion.135
  74.7 1.1 fusion.135
  77.5 1.1 fusion.135
  80.3 1.1 fusion.135
  83.1 1.1 fusion.135
  85.9 1.1 fusion.135
  88.7 1.1 fusion.135
  91.5 8.2 %all-gather = f32[8,1,2048]{2,1,0:T(1,128)S(1)} all-gather(f32[1,1,2048]{2,1,0:T(1,128)S(1)} %reshape.46), channel_id=1, replica_groups=mesh['pts'=8,'cen'=4] {'pts'}, dimensions={0}, use_global_device_ids=true | all-gather | bytes 73728 | tf_op jit(solution)/shard_map/all_gather | solution.py:67
  99.8 8.4 %psum.60 = f32[1024]{0:T(1024)S(1)} all-reduce(f32[1024]{0:T(1024)S(1)} %get-tuple-element.259), channel_id=1, replica_groups=mesh['pts'=8,'cen'=4] {'cen'}, use_global_device_ids=true, to_apply=%region_13.14 | all-reduce | flops 1024 | bytes 8192 | tf_op jit(solution)/shard_map/psum | solution.py:66
  108.2 22.4 %while.71 = (s32[]{:T(128)}, f32[1024]{0:T(1024)S(1)}, f32[8,256]{1,0:T(8,128)S(1)}, f32[1024]{0:T(1024)S(1)}, f32[8,256]{1,0:T(8,128)S(1)}, /*index=5*/f32[8,25...) while((s32[]{:T(128)}, f32[1024]{0:T(1024)S(1)}, ...), condition=%wide.region_15.16_spmd.clone, body=%wide.region_14.15_spmd.clone.sunk | while | flops 208668672 | bytes 3570831 | solution.py:62
  108.2 1.1 fusion.144
  111.0 1.1 fusion.144
  113.8 1.1 fusion.144
  116.6 1.1 fusion.144
  119.4 1.1 fusion.144
  122.2 1.1 fusion.144
  125.0 1.1 fusion.144
  127.8 1.1 fusion.144
  130.6 9.3 %all-gather.1 = f32[8,1,2048]{2,1,0:T(1,128)S(1)} all-gather(f32[1,1,2048]{2,1,0:T(1,128)S(1)} %reshape.48), channel_id=1, replica_groups=mesh['pts'=8,'cen'=4] {'pts'}, dimensions={0}, use_global_device_ids=true | all-gather | bytes 73728 | tf_op jit(solution)/shard_map/all_gather | solution.py:67
  140.0 10.4 %psum.61 = f32[1024]{0:T(1024)S(1)} all-reduce(f32[1024]{0:T(1024)S(1)} %get-tuple-element.261), channel_id=1, replica_groups=mesh['pts'=8,'cen'=4] {'cen'}, use_global_device_ids=true, to_apply=%region_17.18 | all-reduce | flops 1024 | bytes 8192 | tf_op jit(solution)/shard_map/psum | solution.py:66
  150.4 22.4 %while.72 = (s32[]{:T(128)}, f32[1024]{0:T(1024)S(1)}, f32[8,256]{1,0:T(8,128)S(1)}, f32[1024]{0:T(1024)S(1)}, f32[8,256]{1,0:T(8,128)S(1)}, /*index=5*/f32[8,25...) while((s32[]{:T(128)}, f32[1024]{0:T(1024)S(1)}, ...), condition=%wide.region_19.20_spmd.clone, body=%wide.region_18.19_spmd.clone.sunk | while | flops 208668672 | bytes 3570831 | solution.py:62
  150.4 1.1 fusion.153
  153.2 1.1 fusion.153
  156.0 1.1 fusion.153
  158.8 1.1 fusion.153
  161.6 1.1 fusion.153
  164.4 1.1 fusion.153
  167.2 1.1 fusion.153
  170.0 1.1 fusion.153
  172.8 8.4 %psum.62 = f32[1024]{0:T(1024)S(1)} all-reduce(f32[1024]{0:T(1024)S(1)} %get-tuple-element.262), channel_id=1, replica_groups=mesh['pts'=8,'cen'=4] {'cen'}, use_global_device_ids=true, to_apply=%region_21.22 | all-reduce | flops 1024 | bytes 8192 | tf_op jit(solution)/shard_map/psum | solution.py:66
  181.2 8.2 %all-gather.2 = f32[8,1,2048]{2,1,0:T(1,128)S(1)} all-gather(f32[1,1,2048]{2,1,0:T(1,128)S(1)} %reshape.50), channel_id=1, replica_groups=mesh['pts'=8,'cen'=4] {'pts'}, dimensions={0}, use_global_device_ids=true | all-gather | bytes 73728 | tf_op jit(solution)/shard_map/all_gather | solution.py:67
  189.6 40.9 %while.73 = (s32[]{:T(128)}, f32[1024,64]{0,1:T(8,128)S(1)}, f32[8,256,64]{1,0,2:T(8,128)S(1)}, f32[1024]{0:T(1024)S(1)}, f32[8,256]{1,0:T(8,128)S(1)}, /*index=...) while((s32[]{:T(128)}, f32[1024,64]{0,1:T(8,128)S(1)}, ...), condition=%wide.region_23.24_spmd.clone, body=%wide.region_22.23_spmd.clone.sunk | while | flops 807272448 | bytes 7288987 | solution.py:96
  189.6 1.1 fusion.164
  194.7 1.1 fusion.164
  199.8 1.1 fusion.164
  204.9 1.1 fusion.164
  210.0 1.1 fusion.164
  215.1 1.1 fusion.164
  220.2 1.1 fusion.164
  225.3 1.1 fusion.164
  232.2 33.5 %all-reduce.4.cloned.1.call-done = f32[1024,64]{0,1:T(8,128)} async-done(((f32[1024,64]{0,1:T(8,128)}), f32[1024,64]{0,1:T(8,128)}) %all-reduce.4.cloned.1.call-update) | async-done | bytes 262160 | tf_op jit(solution)/shard_map/psum | solution.py:100
  265.6 2.5 reduce-scatter.2.cloned.1.call-done
  268.1 1.7 copy.82
  (249 shorter events, 75.8 us)
Async XLA Ops:
  8.0 257.6 %all-reduce.4.cloned.1.call-start = ((), (), s32[]{:S(2)}) async-start(), calls=%async_computation.1 | async-start | bytes 524288 | tf_op jit(solution)/shard_map/psum | solution.py:100
  8.1 0.7 copy-start.4
  8.8 1.5 copy-start
  8.8 1.5 copy-start.1
  10.2 0.7 copy-start.3
  230.4 0.7 copy-start.2
  231.1 37.0 %reduce-scatter.2.cloned.1.call-start = ((), (), s32[]{:S(2)}) async-start(), calls=%async_computation.2 | async-start | bytes 589824 | tf_op jit(solution)/shard_map/reduce_scatter | solution.py:97
Sparse Core Ops, SparseCore 0:
  231.3 34.3 all-reduce.3
Sparse Core Ops, SparseCore 1:
  235.3 32.8 reduce-scatter.1
